TPU v7x, 32 devices: a whole 2x2x4 slice. The times are simulated.
32 devices in a mesh: gx: 4 (over y, x), gy: 8 (over z, core).
Axes of the slice: x: 2, y: 2, z: 4, core: 2. Of those that a mesh axis runs over, the one named last changes fastest.
Arguments:
- probes: float32 [24, 48, 64, 128], P('gx', 'gy'), may hold values from -6 to 6
- pair_blocks: float32 [24, 48, 9, 128, 128], P('gx', 'gy'), may hold values from -0.09375 to 0.09375
- partners: int32 [24, 48, 9], P('gx', 'gy'), may hold values from 0 to 1151, as said below
- shifts: int32 [2, 24, 48, 9], P(None, 'gx', 'gy'), may hold values from -1 to 1, as said below
- counts: int32 [24, 48], P('gx', 'gy'), may hold values from 1 to 9, as said below
- kpoint: float32 [2], replicated, may hold values from -3.140625 to 3.140625
Outputs:
- last_vector: float32 [24, 48, 64, 128], P('gx', 'gy')
- intersections: float32 [3, 2, 32], replicated
Inputs may be any that keep to these rules, and one draw needn't show every extreme that they name: `partners`: slot 0 of cell (x, y) names the cell itself; slots 1 to 8 name its eight neighbouring cells (x + dx, y + dy) with dx, dy in -1..1 taken periodically modulo 24 and 48, each once, in no fixed order. shifts[0, x, y, s] = (x + dx - px) / 24 and shifts[1, x, y, s] = (y + dy - py) / 48 for the slot's offset (dx, dy) and partner cell (px, py). `counts`: slots at or beyond a cell's count are padding; some cell has all 9 slots live.
All inputs are finite; a program needn't handle non-finite values.
Results may differ from a plain program's by a relative error of at most 0.0001.
Values sent between devices are 32-bit elements; how exact they have to be, the bound alone decides.
A program may use at most 128 MiB of HBM per device.

v0:
```python
import functools
import math

import jax
import jax.numpy as jnp
from jax import lax
from jax.experimental import pallas as pl
from jax.experimental.pallas import tpu as pltpu
from jax.sharding import PartitionSpec as P

STEPS = 3
MESH = pl.DeviceIdType.MESH
F32, BF16 = jnp.float32, jnp.bfloat16


def kernel(
    axes, partners, counts, kpoint, v0_hbm, blocks_hbm, last, total,
    v0, v1, v2, halo_x, halo_y, field_a, field_b, landed, weights, sums, ring_x, ring_y, table, turns,
    v0_sem, land_sem, send_sem, recv_sem, sum_send_x, sum_recv_x, sum_send_y, sum_recv_y,
):
    (name_x, size_x), (name_y, size_y) = axes
    cx, cy, width, block = v0.shape
    slots = landed.shape[1]
    half = width // 2
    pitch = cy + 2
    me_x, me_y = lax.axis_index(name_x), lax.axis_index(name_y)
    total_x, total_y = cx * size_x, cy * size_y
    vectors = (v0, v1, v2, last)
    fields = (field_a, field_b)

    def landing(x, y):
        i = x * cy + y
        return pltpu.make_async_copy(blocks_hbm.at[x, y], landed.at[i], land_sem.at[i])

    inner = (cx - 2) * (cy - 2)
    early = inner // 2

    def interior(k):
        return 1 + k // (cy - 2), 1 + k % (cy - 2)

    def rim_y(k):
        return 1 + k // 2, (k % 2) * (cy - 1)

    def corner(k):
        return (k // 2) * (cx - 1), (k % 2) * (cy - 1)

    def rim_x_near(k):
        return (k // 2) * (cx - 1), 1 + (k % 2) * (cy - 3)

    def rim_x_middle(k):
        return (k // (cy - 4)) * (cx - 1), 2 + k % (cy - 4)

    groups = (
        (interior, early),
        (rim_y, 2 * (cx - 2)),
        (corner, 4),
        (rim_x_near, 4),
        (rim_x_middle, 2 * (cy - 4)),
        (lambda k: interior(k + early), inner - early),
    )
    ends, near, middle = ((0, 1), (cy - 1, 1)), ((1, 1), (cy - 2, 1)), ((2, cy - 4),)

    load_v0 = pltpu.make_async_copy(v0_hbm, v0, v0_sem)
    load_v0.start()
    for place, count in groups:

        @pl.loop(0, count)
        def _(k):
            landing(*place(k)).start()

    barrier = pltpu.get_barrier_semaphore()
    for name, size, me in ((name_x, size_x, me_x), (name_y, size_y, me_y)):
        for j in range(1, size):
            pl.semaphore_signal(
                barrier, inc=1, device_id={name: lax.rem(me + j, size)}, device_id_type=MESH
            )
    pl.semaphore_wait(barrier, size_x + size_y - 2)

    def towards(name, size, me, side):
        return {name: lax.rem(me + (size - 1 if side else 1), size)}

    def remote(step, kind, src, dst, peer):
        return pltpu.make_async_remote_copy(
            src_ref=src,
            dst_ref=dst,
            send_sem=send_sem.at[step, kind],
            recv_sem=recv_sem.at[step, kind],
            device_id=peer,
            device_id_type=MESH,
        )

    def x_copies(step, parts):
        return [
            remote(
                step,
                2 * (ends + near + middle).index((first, length)) + side,
                vectors[step].at[0 if side else cx - 1, pl.ds(first, length)],
                halo_x.at[step, side, pl.ds(first, length)],
                towards(name_x, size_x, me_x, side),
            )
            for first, length in parts
            for side in range(2)
        ]

    def y_copies(step):
        return [
            remote(
                step,
                10 + side,
                vectors[step].at[:, 0 if side else cy - 1],
                halo_y.at[step, side, pl.ds(1, cx)],
                towards(name_y, size_y, me_y, side),
            )
            for side in range(2)
        ]

    def corner_copies(step):
        return [
            remote(
                step,
                12 + 2 * side + end,
                halo_x.at[step, end, 0 if side else cy - 1],
                halo_y.at[step, side, end * (cx + 1)],
                towards(name_y, size_y, me_y, side),
            )
            for side in range(2)
            for end in range(2)
        ]

    def start(copies):
        for copy in copies:
            copy.start()

    def arrive(copies):
        for copy in copies:
            copy.wait_recv()

    def put(field, position, value):
        high = value.astype(BF16)
        field[position, :width] = high
        field[position, width:] = (value - high.astype(F32)).astype(BF16)

    def put_turned(field, position, value, at_x, at_y):
        entry = at_x * 3 + at_y
        cosine, sine = turns[0, entry : entry + 1], turns[1, entry : entry + 1]
        real, imag = value[:half], value[half:]
        put(
            field,
            position,
            jnp.concatenate(
                [cosine * real - sine * imag, sine * real + cosine * imag], axis=0
            ),
        )

    def prepare(x, y):
        i = x * cy + y
        landing(x, y).wait()
        count = counts[x, y]
        for s in range(slots):
            partner = partners[x, y, s]
            partner_x = (partner * (((1 << 20) + total_y - 1) // total_y)) >> 20
            at_x = partner_x - me_x * cx + 1
            at_x = jnp.where(at_x < 0, at_x + total_x, at_x)
            at_x = jnp.where(at_x >= total_x, at_x - total_x, at_x)
            at_y = partner - partner_x * total_y - me_y * cy + 1
            at_y = jnp.where(at_y < 0, at_y + total_y, at_y)
            at_y = jnp.where(at_y >= total_y, at_y - total_y, at_y)
            table[i * slots + s] = at_x * pitch + at_y
            entry = landed[i, s] * jnp.where(s < count, 1.0, 0.0).astype(F32)
            high = entry.astype(BF16)
            weights[i, s * block : (s + 1) * block, :block] = high
            weights[i, s * block : (s + 1) * block, block:] = (
                entry - high.astype(F32)
            ).astype(BF16)

    def advance(step, x, y):
        i = x * cy + y
        source = fields[step % 2]
        final = (cx + 2) * pitch - 1
        lhs = jnp.concatenate(
            [
                source[jnp.minimum(jnp.maximum(table[i * slots + s], 0), final)]
                for s in range(slots)
            ],
            axis=1,
        )
        product = jnp.dot(lhs, weights[i], preferred_element_type=F32)
        value = product[:width, :block] + (
            product[width:, :block] + product[:width, block:] + product[width:, block:]
        )
        if step:
            value = 2.0 * value - vectors[step - 1][x, y]
        vectors[step + 1][x, y] = value
        if step + 1 < STEPS:
            put(fields[(step + 1) % 2], (x + 1) * pitch + y + 1, value)
        start_vector = v0[x, y]
        first_re, first_im = start_vector[:half], start_vector[half:]
        other_re, other_im = value[:half], value[half:]
        low = step * width
        sums[low : low + half] += first_re * other_re + first_im * other_im
        sums[low + half : low + width] += first_re * other_im - first_im * other_re

    def run(step, group):
        place, count = groups[group]

        def body(k, carry):
            x, y = place(k)
            if step == 0:
                prepare(x, y)
            advance(step, x, y)
            return carry

        lax.fori_loop(0, count, body, 0, unroll=1 if step == 0 else 2)

    load_v0.wait()
    start(x_copies(0, ends) + y_copies(0) + x_copies(0, near) + x_copies(0, middle))
    sums[...] = jnp.zeros_like(sums)
    row = lax.broadcasted_iota(jnp.int32, (16, block), 0)

    def crossing(at, me, size):
        low = (at == 0) & (me == 0)
        high = (at == 2) & (me == size - 1)
        return jnp.where(low, -1.0, jnp.where(high, 1.0, 0.0)).astype(F32)

    angle = kpoint[0] * crossing(row // 3, me_x, size_x)
    angle = angle + kpoint[1] * crossing(row % 3, me_y, size_y)
    turns[0], turns[1] = jnp.cos(angle), jnp.sin(angle)

    @pl.loop(0, cx * cy)
    def _(k):
        x, y = k // cy, k % cy
        put(field_a, (x + 1) * pitch + y + 1, v0[x, y])

    def put_x(step, parts):
        for first, length in parts:
            for y in range(first, first + length):
                for side in range(2):
                    put_turned(
                        fields[step % 2],
                        side * (cx + 1) * pitch + y + 1,
                        halo_x[step, side, y],
                        2 * side,
                        1,
                    )

    for step in range(STEPS):
        field = fields[step % 2]
        more = step + 1 < STEPS
        run(step, 0)
        if not more:
            run(step, 5)
        arrive(x_copies(step, ends))
        start(corner_copies(step))
        put_x(step, ends)
        arrive(y_copies(step))
        for side in range(2):

            @pl.loop(0, cx)
            def _(x):
                put_turned(
                    field,
                    (x + 1) * pitch + side * (cy + 1),
                    halo_y[step, side, x + 1],
                    1,
                    2 * side,
                )

        run(step, 1)
        arrive(x_copies(step, near))
        put_x(step, near)
        arrive(corner_copies(step))
        for side in range(2):
            for end in range(2):
                put_turned(
                    field,
                    end * (cx + 1) * pitch + side * (cy + 1),
                    halo_y[step, side, end * (cx + 1)],
                    2 * end,
                    2 * side,
                )
        run(step, 2)
        if more:
            start(x_copies(step + 1, ends) + y_copies(step + 1))
        arrive(x_copies(step, middle))
        put_x(step, middle)
        run(step, 3)
        if more:
            start(x_copies(step + 1, near))
        run(step, 4)
        if more:
            start(x_copies(step + 1, middle))
            run(step, 5)

    found = lax.dot_general(
        jnp.ones((8, block), F32),
        sums[...],
        (((1,), (1,)), ((), ())),
        precision=lax.Precision.HIGHEST,
        preferred_element_type=F32,
    )
    for name, size, me, ring, sent, got in (
        (name_x, size_x, me_x, ring_x, sum_send_x, sum_recv_x),
        (name_y, size_y, me_y, ring_y, sum_send_y, sum_recv_y),
    ):
        ring[me] = found
        copies = [
            pltpu.make_async_remote_copy(
                src_ref=ring.at[me],
                dst_ref=ring.at[me],
                send_sem=sent.at[j],
                recv_sem=got.at[j],
                device_id={name: lax.rem(me + j, size)},
                device_id_type=MESH,
            )
            for j in range(1, size)
        ]
        start(copies)
        for copy in copies:
            copy.wait()
        found = ring[0]
        for j in range(1, size):
            found = found + ring[j]
    total[...] = found
    for step in range(STEPS):
        for copy in (
            x_copies(step, ends + near + middle) + y_copies(step) + corner_copies(step)
        ):
            copy.wait_send()


def shards(axes, probes, pair_blocks, partners, shifts, counts, kpoint):
    (name_x, size_x), (name_y, size_y) = axes
    cx, cy, width, block = probes.shape
    slots = pair_blocks.shape[2]
    cells = cx * cy
    total_x, total_y = cx * size_x, cy * size_y
    rows = STEPS * width
    halo = (width, block)
    smem = pl.BlockSpec(memory_space=pltpu.SMEM)
    anywhere = pl.BlockSpec(memory_space=pl.ANY)
    vmem = pl.BlockSpec(memory_space=pltpu.VMEM)
    dma = pltpu.SemaphoreType.DMA
    last, found = pl.pallas_call(
        functools.partial(kernel, axes),
        out_shape=(
            jax.ShapeDtypeStruct(probes.shape, F32),
            jax.ShapeDtypeStruct((8, rows), F32),
        ),
        in_specs=[smem, smem, smem, anywhere, anywhere],
        out_specs=(vmem, vmem),
        scratch_shapes=[
            pltpu.VMEM(probes.shape, F32),
            pltpu.VMEM(probes.shape, F32),
            pltpu.VMEM(probes.shape, F32),
            pltpu.VMEM((STEPS, 2, cy) + halo, F32),
            pltpu.VMEM((STEPS, 2, cx + 2) + halo, F32),
            pltpu.VMEM(((cx + 2) * (cy + 2), 2 * width, block), BF16),
            pltpu.VMEM(((cx + 2) * (cy + 2), 2 * width, block), BF16),
            pltpu.VMEM((cells, slots, block, block), F32),
            pltpu.VMEM((cells, slots * block, 2 * block), BF16),
            pltpu.VMEM((rows, block), F32),
            pltpu.VMEM((size_x, 8, rows), F32),
            pltpu.VMEM((size_y, 8, rows), F32),
            pltpu.SMEM((cells * slots,), jnp.int32),
            pltpu.VMEM((2, 16, block), F32),
            dma(()),
            dma((cells,)),
            dma((STEPS, 16)),
            dma((STEPS, 16)),
            dma((size_x,)),
            dma((size_x,)),
            dma((size_y,)),
            dma((size_y,)),
        ],
        compiler_params=pltpu.CompilerParams(
            collective_id=0, has_side_effects=True, vmem_limit_bytes=66_000_000
        ),
    )(partners, counts, kpoint, probes, pair_blocks)
    scale = 1.0 / math.sqrt(total_x * total_y * block)
    return last, (found[0] * scale).reshape(STEPS, 2, width // 2)


def solution(mesh):
    placed = (
        P("gx", "gy", None, None),
        P("gx", "gy", None, None, None),
        P("gx", "gy", None),
        P(None, "gx", "gy", None),
        P("gx", "gy"),
        P(),
    )
    axes = tuple((name, mesh.shape[name]) for name in ("gx", "gy"))
    return jax.shard_map(
        functools.partial(shards, axes),
        mesh=mesh,
        in_specs=placed,
        out_specs=(P("gx", "gy", None, None), P()),
        check_vma=False,
    )
```

profile of v0, /device:TPU:0, one launch (start us, length us, event | category | flops | bytes accessed | tf_op | source)
XLA Modules:
  0.0 55.5 jit_solution(1789553448188857623)
XLA Ops:
  0.6 51.1 %shard_map.68 = (f32[6,6,64,128]{3,2,1,0:T(8,128)}, f32[8,192]{1,0:T(8,128)}) custom-call(s32[6,6,9]{2,1,0:T(8,128)} %partners.1, s32[6,6]{1,0:T(8,128)} %counts.1, f32[2]{0:T(128)} %kpoint.1, f32[6,6,64,128]{3,2,1,0:T(8,128)} %v0_hbm.1, f32[6,6,9,128,128]{4,3,2,1,0:T(8,128)} %blocks_hbm.1), custom_call_target="tpu_custom_call" | custom-call | tf_op jit(solution)/shard_map/pallas_call | solution.py:343
  51.8 0.7 %multiply_reduce_fusion = f32[192]{0:T(256)S(1)} fusion(f32[8,192]{1,0:T(8,128)} %get-tuple-element.5), kind=kLoop, calls=%fused_computation | loop fusion | flops 192 | bytes 1536 | tf_op jit(solution)/shard_map/mul | solution.py:380
  52.5 0.7 %mul.12 = f32[3,2,32]{2,1,0:T(2,128)} reshape(f32[192]{0:T(256)S(1)} %multiply_reduce_fusion) | data formatting | bytes 1536 | tf_op jit(solution)/shard_map/mul | solution.py:380
  53.1 2.4 %copy.8 = f32[6,6,64,128]{3,2,1,0:T(8,128)} copy(f32[6,6,64,128]{3,2,1,0:T(8,128)} %get-tuple-element.8) | data formatting | bytes 2359296
where the time goes:
time: 55.8 us; the launch traced here: 55.5 us
  Pallas kernels  51.1 us (92%)
  local copies, waits for them, and re-layouts  3.07 us (6%)
  other arithmetic  0.72 us (1%)
  between operations  0.64 us (1%)
    pallas_call x1, Pallas kernels, shards(): pl.pallas_call(functools.partial(kernel, axes), out_shape=(jax.ShapeDtype...  51.1 us
    unnamed x1, local copies, waits for them, and re-layouts  2.41 us

commit v1 on v0

v1 whole, which is shorter than its diff:
```python
import functools
import math

import jax
import jax.numpy as jnp
from jax import lax
from jax.experimental import pallas as pl
from jax.experimental.pallas import tpu as pltpu
from jax.sharding import PartitionSpec as P

STEPS = 3
MESH = pl.DeviceIdType.MESH
F32, BF16 = jnp.float32, jnp.bfloat16


def kernel(
    axes, partners, counts, kpoint, v0_hbm, blocks_hbm, last, total,
    v0, v1, v2, halo_x, halo_y, field_a, field_b, landed, upper, lower, sums, ring_x, ring_y, table, turns,
    v0_sem, land_sem, send_sem, recv_sem, sum_send_x, sum_recv_x, sum_send_y, sum_recv_y,
):
    (name_x, size_x), (name_y, size_y) = axes
    cx, cy, width, block = v0.shape
    slots = landed.shape[1]
    half = width // 2
    pitch = cy + 2
    nothing = (cx + 2) * pitch
    me_x, me_y = lax.axis_index(name_x), lax.axis_index(name_y)
    total_x, total_y = cx * size_x, cy * size_y
    vectors = (v0, v1, v2, last)
    fields = (field_a, field_b)

    def landing(x, y):
        i = x * cy + y
        return pltpu.make_async_copy(blocks_hbm.at[x, y], landed.at[i], land_sem.at[i])

    inner = (cx - 2) * (cy - 2)

    def interior(k):
        return 1 + k // (cy - 2), 1 + k % (cy - 2)

    def rim_y(k):
        return 1 + k // 2, (k % 2) * (cy - 1)

    def mirror(step, y):
        return cy - 1 - y if step % 2 else y

    def rim_x(step, ys):
        return lambda k: ((k % 2) * (cx - 1), mirror(step, ys[k // 2]))

    wire = (0, cy - 1, cy - 2) + tuple(range(1, cy - 2))
    ready = ((cy - 1,), (0,)) + tuple((p - 1,) for p in range(2, cy - 3))
    ready = ready + ((cy - 4, cy - 3, cy - 2),)
    early = inner // 2

    for signal_name, size, me in ((name_x, size_x, me_x), (name_y, size_y, me_y)):
        for j in range(1, size):
            pl.semaphore_signal(
                pltpu.get_barrier_semaphore(),
                inc=1,
                device_id={signal_name: lax.rem(me + j, size)},
                device_id_type=MESH,
            )
    load_v0 = pltpu.make_async_copy(v0_hbm, v0, v0_sem)
    load_v0.start()
    for place, count in (
        (interior, inner),
        (rim_y, 2 * (cx - 2)),
        *((rim_x(0, ys), 2 * len(ys)) for ys in ready),
    ):
        if count > 6:

            @pl.loop(0, count)
            def _(k):
                landing(*place(k)).start()
        else:
            for k in range(count):
                landing(*place(k)).start()
    pl.semaphore_wait(pltpu.get_barrier_semaphore(), size_x + size_y - 2)

    def towards(name, size, me, side):
        return {name: lax.rem(me + (size - 1 if side else 1), size)}

    def remote(step, kind, src, dst, peer):
        return pltpu.make_async_remote_copy(
            src_ref=src,
            dst_ref=dst,
            send_sem=send_sem.at[step, kind],
            recv_sem=recv_sem.at[step, kind],
            device_id=peer,
            device_id_type=MESH,
        )

    def source(step):
        return vectors[step] if step else v0_hbm

    def x_copies(step, y):
        return [
            remote(
                step,
                2 * y + side,
                source(step).at[0 if side else cx - 1, y],
                halo_x.at[step, side, y],
                towards(name_x, size_x, me_x, side),
            )
            for side in range(2)
        ]

    def y_copy(step, side, x, length):
        return remote(
            step,
            2 * cy + 3 * side + (0 if x == 0 else 1 if x == 1 else 2),
            source(step).at[pl.ds(x, length), 0 if side else cy - 1],
            halo_y.at[step, side, pl.ds(1 + x, length)],
            towards(name_y, size_y, me_y, side),
        )

    def y_middles(step):
        return [y_copy(step, side, 1, cx - 2) for side in range(2)]

    def y_ends(step, side):
        return [y_copy(step, side, x, 1) for x in (0, cx - 1)]

    def corner_copies(step, side):
        return [
            remote(
                step,
                2 * cy + 6 + 2 * side + end,
                halo_x.at[step, end, 0 if side else cy - 1],
                halo_y.at[step, side, end * (cx + 1)],
                towards(name_y, size_y, me_y, side),
            )
            for end in range(2)
        ]

    def start(copies):
        for copy in copies:
            copy.start()

    def arrive(copies):
        for copy in copies:
            copy.wait_recv()

    def put(field, position, value):
        high = value.astype(BF16)
        field[position, :width] = high
        field[position, width:] = (value - high.astype(F32)).astype(BF16)

    def put_turned(field, position, value, at_x, at_y):
        entry = at_x * 3 + at_y
        cosine, sine = turns[0, entry : entry + 1], turns[1, entry : entry + 1]
        real, imag = value[:half], value[half:]
        put(
            field,
            position,
            jnp.concatenate(
                [cosine * real - sine * imag, sine * real + cosine * imag], axis=0
            ),
        )

    def put_x(step, y):
        for side in range(2):
            put_turned(
                fields[step % 2],
                side * (cx + 1) * pitch + y + 1,
                halo_x[step, side, y],
                2 * side,
                1,
            )

    def put_y(step, side, x, at_x):
        put_turned(
            fields[step % 2],
            x * pitch + side * (cy + 1),
            halo_y[step, side, x],
            at_x,
            2 * side,
        )

    def prepare(x, y):
        i = x * cy + y
        count = counts[x, y]
        for s in range(slots):
            partner = partners[x, y, s]
            partner_x = (partner * (((1 << 20) + total_y - 1) // total_y)) >> 20
            at_x = partner_x - me_x * cx + 1
            at_x = jnp.where(at_x < 0, at_x + total_x, at_x)
            at_x = jnp.where(at_x >= total_x, at_x - total_x, at_x)
            at_y = partner - partner_x * total_y - me_y * cy + 1
            at_y = jnp.where(at_y < 0, at_y + total_y, at_y)
            at_y = jnp.where(at_y >= total_y, at_y - total_y, at_y)
            at = jnp.minimum(jnp.maximum(at_x * pitch + at_y, 0), nothing - 1)
            table[i * slots + s] = jnp.where(s < count, at, nothing)
            entry = landed[i, s]
            high = entry.astype(BF16)
            upper[i, s * block : (s + 1) * block] = high
            lower[i, s * block : (s + 1) * block] = (
                entry - high.astype(F32)
            ).astype(BF16)

    def advance(step, x, y):
        i = x * cy + y
        field = fields[step % 2]
        lhs = jnp.concatenate(
            [
                field[jnp.minimum(jnp.maximum(table[i * slots + s], 0), nothing)]
                for s in range(slots)
            ],
            axis=1,
        )
        rhs = jnp.concatenate([upper[i], lower[i]], axis=1)
        product = jnp.dot(lhs, rhs, preferred_element_type=F32)
        value = product[:width, :block] + (
            product[width:, :block] + product[:width, block:] + product[width:, block:]
        )
        if step:
            value = 2.0 * value - vectors[step - 1][x, y]
        vectors[step + 1][x, y] = value
        if step + 1 < STEPS:
            put(fields[(step + 1) % 2], (x + 1) * pitch + y + 1, value)
        start_vector = v0[x, y]
        first_re, first_im = start_vector[:half], start_vector[half:]
        other_re, other_im = value[:half], value[half:]
        return (
            first_re * other_re + first_im * other_im,
            first_re * other_im - first_im * other_re,
        )

    def run(step, place, first, count, unroll):
        def body(k):
            cells = [place(first + k * unroll + u) for u in range(unroll)]
            if step == 0:
                for x, y in cells:
                    landing(x, y).wait()
            found = []
            for x, y in cells:
                if step == 0:
                    prepare(x, y)
                found.append(advance(step, x, y))
            low = step * width
            sums[low : low + half] += sum(real for real, _ in found)
            sums[low + half : low + width] += sum(imag for _, imag in found)

        if count == unroll:
            body(0)
        else:
            pl.loop(0, count // unroll)(body)

    for y in wire:
        start(x_copies(0, y))
    start(y_middles(0) + y_ends(0, 0) + y_ends(0, 1))
    sums[...] = jnp.zeros_like(sums)
    for field in fields:
        field[nothing] = jnp.zeros_like(field[nothing])
    row = lax.broadcasted_iota(jnp.int32, (16, block), 0)

    def crossing(at, me, size):
        low = (at == 0) & (me == 0)
        high = (at == 2) & (me == size - 1)
        return jnp.where(low, -1.0, jnp.where(high, 1.0, 0.0)).astype(F32)

    angle = kpoint[0] * crossing(row // 3, me_x, size_x)
    angle = angle + kpoint[1] * crossing(row % 3, me_y, size_y)
    turns[0], turns[1] = jnp.cos(angle), jnp.sin(angle)
    load_v0.wait()

    @pl.loop(0, cx * cy)
    def _(k):
        x, y = k // cy, k % cy
        put(field_a, (x + 1) * pitch + y + 1, v0[x, y])

    for step in range(STEPS):
        more = step + 1 < STEPS
        order = [mirror(step, y) for y in wire]
        near = 1 if step % 2 else 0
        run(step, interior, 0, early, 4)
        arrive(x_copies(step, order[0]))
        start(corner_copies(step, 1 - near))
        run(step, interior, early, inner - early, 4)
        arrive(x_copies(step, order[1]))
        start(corner_copies(step, near))
        put_x(step, order[0])
        put_x(step, order[1])
        arrive(y_middles(step) + y_ends(step, 0) + y_ends(step, 1))
        for side in range(2):

            @pl.loop(0, cx)
            def _(x):
                put_y(step, side, x + 1, 1)

        run(step, rim_y, 0, 2 * (cx - 2), 4)
        if more:
            start(y_middles(step + 1))
        for group, ys in enumerate(ready):
            arrive(x_copies(step, order[group + 2]))
            put_x(step, order[group + 2])
            if group < 2:
                side = 1 - near if group == 0 else near
                arrive(corner_copies(step, side))
                for end in range(2):
                    put_y(step, side, end * (cx + 1), 2 * end)
            run(step, rim_x(step, ys), 0, 2 * len(ys), 2 * len(ys))
            if more:
                if len(ys) > 1:
                    ys = ys[::-1]
                for y in ys:
                    start(x_copies(step + 1, mirror(step, y)))
                if group < 2:
                    start(y_ends(step + 1, 1 if mirror(step, ys[0]) == 0 else 0))

    found = lax.dot_general(
        jnp.ones((8, block), F32),
        sums[...],
        (((1,), (1,)), ((), ())),
        precision=lax.Precision.HIGHEST,
        preferred_element_type=F32,
    )[0:1]
    for name, size, me, ring, sent, got in (
        (name_x, size_x, me_x, ring_x, sum_send_x, sum_recv_x),
        (name_y, size_y, me_y, ring_y, sum_send_y, sum_recv_y),
    ):
        ring[me] = found
        copies = [
            pltpu.make_async_remote_copy(
                src_ref=ring.at[me],
                dst_ref=ring.at[me],
                send_sem=sent.at[j],
                recv_sem=got.at[j],
                device_id={name: lax.rem(me + j, size)},
                device_id_type=MESH,
            )
            for j in range(1, size)
        ]
        start(copies)
        for copy in copies:
            copy.wait()
        found = ring[0]
        for j in range(1, size):
            found = found + ring[j]
    total[...] = found
    for step in range(STEPS):
        for y in wire:
            for copy in x_copies(step, y):
                copy.wait_send()
        for side in range(2):
            for copy in y_ends(step, side) + corner_copies(step, side):
                copy.wait_send()
        for copy in y_middles(step):
            copy.wait_send()


def shards(axes, probes, pair_blocks, partners, shifts, counts, kpoint):
    (name_x, size_x), (name_y, size_y) = axes
    cx, cy, width, block = probes.shape
    slots = pair_blocks.shape[2]
    cells = cx * cy
    total_x, total_y = cx * size_x, cy * size_y
    rows = STEPS * width
    halo = (width, block)
    smem = pl.BlockSpec(memory_space=pltpu.SMEM)
    anywhere = pl.BlockSpec(memory_space=pl.ANY)
    vmem = pl.BlockSpec(memory_space=pltpu.VMEM)
    dma = pltpu.SemaphoreType.DMA
    kinds = 2 * cy + 10
    last, found = pl.pallas_call(
        functools.partial(kernel, axes),
        out_shape=(
            jax.ShapeDtypeStruct(probes.shape, F32),
            jax.ShapeDtypeStruct((1, rows), F32),
        ),
        in_specs=[smem, smem, smem, anywhere, anywhere],
        out_specs=(vmem, vmem),
        scratch_shapes=[
            pltpu.VMEM(probes.shape, F32),
            pltpu.VMEM(probes.shape, F32),
            pltpu.VMEM(probes.shape, F32),
            pltpu.VMEM((STEPS, 2, cy) + halo, F32),
            pltpu.VMEM((STEPS, 2, cx + 2) + halo, F32),
            pltpu.VMEM(((cx + 2) * (cy + 2) + 1, 2 * width, block), BF16),
            pltpu.VMEM(((cx + 2) * (cy + 2) + 1, 2 * width, block), BF16),
            pltpu.VMEM((cells, slots, block, block), F32),
            pltpu.VMEM((cells, slots * block, block), BF16),
            pltpu.VMEM((cells, slots * block, block), BF16),
            pltpu.VMEM((rows, block), F32),
            pltpu.VMEM((size_x, 1, rows), F32),
            pltpu.VMEM((size_y, 1, rows), F32),
            pltpu.SMEM((cells * slots,), jnp.int32),
            pltpu.VMEM((2, 16, block), F32),
            dma(()),
            dma((cells,)),
            dma((STEPS, kinds)),
            dma((STEPS, kinds)),
            dma((size_x,)),
            dma((size_x,)),
            dma((size_y,)),
            dma((size_y,)),
        ],
        compiler_params=pltpu.CompilerParams(
            collective_id=0, has_side_effects=True, vmem_limit_bytes=66_000_000
        ),
    )(partners, counts, kpoint, probes, pair_blocks)
    scale = 1.0 / math.sqrt(total_x * total_y * block)
    return last, (found[0] * scale).reshape(STEPS, 2, width // 2)


def solution(mesh):
    placed = (
        P("gx", "gy", None, None),
        P("gx", "gy", None, None, None),
        P("gx", "gy", None),
        P(None, "gx", "gy", None),
        P("gx", "gy"),
        P(),
    )
    axes = tuple((name, mesh.shape[name]) for name in ("gx", "gy"))
    return jax.shard_map(
        functools.partial(shards, axes),
        mesh=mesh,
        in_specs=placed,
        out_specs=(P("gx", "gy", None, None), P()),
        check_vma=False,
    )
```

time: 55.8 us -> 49.4 us (0.89)
  Pallas kernels: 51.1 us -> 44.7 us
    pallas_call x1, Pallas kernels: 51.1 us -> 44.7 us  [shards(): pl.pallas_call(functools.partial(kernel, axes), out_shape=(jax.ShapeDtype...]
where the time goes in v1:
time: 49.4 us; the launch traced here: 49.1 us
  Pallas kernels  44.7 us (90%)
  local copies, waits for them, and re-layouts  3.07 us (6%)
  other arithmetic  0.68 us (1%)
  between operations  0.64 us (1%)
    pallas_call x1, Pallas kernels, shards(): pl.pallas_call(functools.partial(kernel, axes), out_shape=(jax.ShapeDtype...  44.7 us
    unnamed x1, local copies, waits for them, and re-layouts  2.41 us

profile of v1, /device:TPU:0, one launch (start us, length us, event | category | flops | bytes accessed | tf_op | source)
XLA Modules:
  0.0 49.1 jit_solution(18169640682311021427)
XLA Ops:
  0.6 44.7 %shard_map.68 = (f32[6,6,64,128]{3,2,1,0:T(8,128)}, f32[1,192]{1,0:T(1,128)}) custom-call(s32[6,6,9]{2,1,0:T(8,128)} %partners.1, s32[6,6]{1,0:T(8,128)} %counts.1, f32[2]{0:T(128)} %kpoint.1, f32[6,6,64,128]{3,2,1,0:T(8,128)} %v0_hbm.1, f32[6,6,9,128,128]{4,3,2,1,0:T(8,128)} %blocks_hbm.1), custom_call_target="tpu_custom_call" | custom-call | tf_op jit(solution)/shard_map/pallas_call | solution.py:364
  45.3 0.7 %multiply_reduce_fusion = f32[192]{0:T(256)S(1)} fusion(f32[1,192]{1,0:T(1,128)} %get-tuple-element.5), kind=kLoop, calls=%fused_computation | loop fusion | flops 192 | bytes 1536 | tf_op jit(solution)/shard_map/mul | solution.py:402
  46.0 0.7 %mul.12 = f32[3,2,32]{2,1,0:T(2,128)} reshape(f32[192]{0:T(256)S(1)} %multiply_reduce_fusion) | data formatting | bytes 1536 | tf_op jit(solution)/shard_map/mul | solution.py:402
  46.7 2.4 %copy.8 = f32[6,6,64,128]{3,2,1,0:T(8,128)} copy(f32[6,6,64,128]{3,2,1,0:T(8,128)} %get-tuple-element.8) | data formatting | bytes 2359296

commit v2 on v1

--- a/solution.py
+++ b/solution.py
@@ -14,9 +14,9 @@
 
 
 def kernel(
-    axes, partners, counts, kpoint, v0_hbm, blocks_hbm, last, total,
-    v0, v1, v2, halo_x, halo_y, field_a, field_b, landed, upper, lower, sums, ring_x, ring_y, table, turns,
-    v0_sem, land_sem, send_sem, recv_sem, sum_send_x, sum_recv_x, sum_send_y, sum_recv_y,
+    axes, partners_hbm, counts_hbm, kpoint_hbm, v0_hbm, blocks_hbm, last, total,
+    partners, counts, kpoint, v0, v1, v2, halo_x, halo_y, field_a, field_b, landed, upper, lower, sums, ring_x, ring_y, table, turns,
+    v0_sem, small_sem, land_sem, send_sem, recv_sem, sum_send_x, sum_recv_x, sum_send_y, sum_recv_y,
 ):
     (name_x, size_x), (name_y, size_y) = axes
     cx, cy, width, block = v0.shape
@@ -62,6 +62,14 @@
             )
     load_v0 = pltpu.make_async_copy(v0_hbm, v0, v0_sem)
     load_v0.start()
+    small = [
+        pltpu.make_async_copy(there, here, small_sem.at[i])
+        for i, (there, here) in enumerate(
+            ((partners_hbm, partners), (counts_hbm, counts), (kpoint_hbm, kpoint))
+        )
+    ]
+    for copy in small:
+        copy.start()
     for place, count in (
         (interior, inner),
         (rim_y, 2 * (cx - 2)),
@@ -252,6 +260,8 @@
     for field in fields:
         field[nothing] = jnp.zeros_like(field[nothing])
     row = lax.broadcasted_iota(jnp.int32, (16, block), 0)
+    for copy in small:
+        copy.wait()
 
     def crossing(at, me, size):
         low = (at == 0) & (me == 0)
@@ -348,6 +358,22 @@
             copy.wait_send()
 
 
+def finish(scale, last, found, out, total, sem):
+    copies = [
+        pltpu.make_async_copy(last.at[x], out.at[x], sem.at[x])
+        for x in range(last.shape[0])
+    ]
+    for copy in copies:
+        copy.start()
+    half = total.shape[2]
+    for step in range(STEPS):
+        for part in range(2):
+            low = (2 * step + part) * half
+            total[step, part : part + 1] = found[:, low : low + half] * scale
+    for copy in copies:
+        copy.wait()
+
+
 def shards(axes, probes, pair_blocks, partners, shifts, counts, kpoint):
     (name_x, size_x), (name_y, size_y) = axes
     cx, cy, width, block = probes.shape
@@ -356,20 +382,22 @@
     total_x, total_y = cx * size_x, cy * size_y
     rows = STEPS * width
     halo = (width, block)
-    smem = pl.BlockSpec(memory_space=pltpu.SMEM)
-    anywhere = pl.BlockSpec(memory_space=pl.ANY)
+    hbm = pl.BlockSpec(memory_space=pltpu.HBM)
     vmem = pl.BlockSpec(memory_space=pltpu.VMEM)
     dma = pltpu.SemaphoreType.DMA
     kinds = 2 * cy + 10
     last, found = pl.pallas_call(
         functools.partial(kernel, axes),
         out_shape=(
-            jax.ShapeDtypeStruct(probes.shape, F32),
-            jax.ShapeDtypeStruct((1, rows), F32),
+            pltpu.VMEM(probes.shape, F32),
+            pltpu.VMEM((1, rows), F32),
         ),
-        in_specs=[smem, smem, smem, anywhere, anywhere],
+        in_specs=[hbm] * 5,
         out_specs=(vmem, vmem),
         scratch_shapes=[
+            pltpu.SMEM(partners.shape, jnp.int32),
+            pltpu.SMEM(counts.shape, jnp.int32),
+            pltpu.SMEM(kpoint.shape, F32),
             pltpu.VMEM(probes.shape, F32),
             pltpu.VMEM(probes.shape, F32),
             pltpu.VMEM(probes.shape, F32),
@@ -386,6 +414,7 @@
             pltpu.SMEM((cells * slots,), jnp.int32),
             pltpu.VMEM((2, 16, block), F32),
             dma(()),
+            dma((3,)),
             dma((cells,)),
             dma((STEPS, kinds)),
             dma((STEPS, kinds)),
@@ -395,11 +424,20 @@
             dma((size_y,)),
         ],
         compiler_params=pltpu.CompilerParams(
-            collective_id=0, has_side_effects=True, vmem_limit_bytes=66_000_000
+            collective_id=0, has_side_effects=True, vmem_limit_bytes=60_000_000
         ),
     )(partners, counts, kpoint, probes, pair_blocks)
     scale = 1.0 / math.sqrt(total_x * total_y * block)
-    return last, (found[0] * scale).reshape(STEPS, 2, width // 2)
+    return pl.pallas_call(
+        functools.partial(finish, scale),
+        out_shape=(
+            jax.ShapeDtypeStruct(probes.shape, F32),
+            jax.ShapeDtypeStruct((STEPS, 2, width // 2), F32),
+        ),
+        in_specs=[vmem, vmem],
+        out_specs=(hbm, vmem),
+        scratch_shapes=[dma((cx,))],
+    )(*(pltpu.with_memory_space_constraint(part, pltpu.VMEM) for part in (last, found)))
 
 
 def solution(mesh):

time: 49.4 us -> 45 us (0.911)
  local copies, waits for them, and re-layouts: 3.07 us -> 0 us
  other arithmetic: 0.68 us -> 0 us
  Pallas kernels: 44.7 us -> 44.2 us
    unnamed x1 -> x0, local copies, waits for them, and re-layouts: 2.41 us -> none
    mul x1 -> x0, other arithmetic: 0.68 us -> none  [shards(): return (last, (found[0] * scale).reshape(STEPS, 2, width // 2))]
    mul x1 -> x0, local copies, waits for them, and re-layouts: 0.66 us -> none  [shards(): return (last, (found[0] * scale).reshape(STEPS, 2, width // 2))]
    pallas_call x1 -> x2, Pallas kernels: 44.7 us -> 44.2 us  [the longest x1 42.6 us: shards(): pl.pallas_call(functools.partial(kernel, axes), out_shape=(pltpu.VMEM(pro...]
where the time goes in v2:
time: 45 us; the launch traced here: 44.9 us
  Pallas kernels  44.2 us (98%)
  between operations  0.64 us (1%)
    pallas_call x1, Pallas kernels, shards(): pl.pallas_call(functools.partial(kernel, axes), out_shape=(pltpu.VMEM(pro...  42.6 us
    pallas_call x1, Pallas kernels, shards(): pl.pallas_call(functools.partial(finish, scale), out_shape=(jax.ShapeDtyp...  1.63 us

profile of v2, /device:TPU:0, one launch (start us, length us, event | category | flops | bytes accessed | tf_op | source)
XLA Modules:
  0.0 44.9 jit_solution(12246778680784204842)
XLA Ops:
  0.6 42.6 %shard_map.68 = (f32[6,6,64,128]{3,2,1,0:T(8,128)S(1)}, f32[1,192]{1,0:T(1,128)S(1)}) custom-call(s32[6,6,9]{2,1,0:T(8,128)} %partners_hbm.1, s32[6,6]{1,0:T(8,128)} %counts_hbm.1, f32[2]{0:T(128)} %kpoint_hbm.1, f32[6,6,64,128]{3,2,1,0:T(8,128)} %v0_hbm.1, f32[6,6,9,128,128]{4,3,2,1,0:T(8,128)} %blocks_hbm.1), custom_call_target="tpu_custom_call" | custom-call | tf_op jit(solution)/shard_map/pallas_call | solution.py:389
  43.3 1.6 %shard_map.69 = (f32[6,6,64,128]{3,2,1,0:T(8,128)}, f32[3,2,32]{2,1,0:T(2,128)}) custom-call(f32[6,6,64,128]{3,2,1,0:T(8,128)S(1)} %get-tuple-element.4.last, f32[1,192]{1,0:T(1,128)S(1)} %get-tuple-element.5.found), custom_call_target="tpu_custom_call" | custom-call | tf_op jit(solution)/shard_map/pallas_call | solution.py:431

commit v3 on v2

--- a/solution.py
+++ b/solution.py
@@ -15,7 +15,7 @@
 
 def kernel(
     axes, partners_hbm, counts_hbm, kpoint_hbm, v0_hbm, blocks_hbm, last, total,
-    partners, counts, kpoint, v0, v1, v2, halo_x, halo_y, field_a, field_b, landed, upper, lower, sums, ring_x, ring_y, table, turns,
+    partners, counts, kpoint, v0, v1, v2, halo_x, halo_y, field_a, field_b, landed, upper, lower, sums, ring_x, ring_y, table, sooner, late, turns,
     v0_sem, small_sem, land_sem, send_sem, recv_sem, sum_send_x, sum_recv_x, sum_send_y, sum_recv_y,
 ):
     (name_x, size_x), (name_y, size_y) = axes
@@ -50,6 +50,8 @@
     wire = (0, cy - 1, cy - 2) + tuple(range(1, cy - 2))
     ready = ((cy - 1,), (0,)) + tuple((p - 1,) for p in range(2, cy - 3))
     ready = ready + ((cy - 4, cy - 3, cy - 2),)
+    final = [rim_x(STEPS - 1, ready[-1])(k) for k in range(2 * len(ready[-1]))]
+    final_y = mirror(STEPS - 1, wire[-1])
     early = inner // 2
 
     for signal_name, size, me in ((name_x, size_x, me_x), (name_y, size_y, me_y)):
@@ -148,6 +150,15 @@
         for copy in copies:
             copy.wait_recv()
 
+    def row_sums(first, length):
+        return lax.dot_general(
+            jnp.ones((8, block), F32),
+            sums[first : first + length],
+            (((1,), (1,)), ((), ())),
+            precision=lax.Precision.HIGHEST,
+            preferred_element_type=F32,
+        )[0:1]
+
     def put(field, position, value):
         high = value.astype(BF16)
         field[position, :width] = high
@@ -187,44 +198,58 @@
     def prepare(x, y):
         i = x * cy + y
         count = counts[x, y]
+        closing = isinstance(y, int) and (x, y) in final
+        late_slot, late_place = jnp.int32(0), jnp.int32(nothing)
+        from_x = lax.rem(me_x * cx + total_x - 1, total_x)
+        from_y = lax.rem(me_y * cy + total_y - 1, total_y)
         for s in range(slots):
             partner = partners[x, y, s]
             partner_x = (partner * (((1 << 20) + total_y - 1) // total_y)) >> 20
-            at_x = partner_x - me_x * cx + 1
+            at_x = partner_x - from_x
             at_x = jnp.where(at_x < 0, at_x + total_x, at_x)
-            at_x = jnp.where(at_x >= total_x, at_x - total_x, at_x)
-            at_y = partner - partner_x * total_y - me_y * cy + 1
+            at_y = partner - partner_x * total_y - from_y
             at_y = jnp.where(at_y < 0, at_y + total_y, at_y)
-            at_y = jnp.where(at_y >= total_y, at_y - total_y, at_y)
-            at = jnp.minimum(jnp.maximum(at_x * pitch + at_y, 0), nothing - 1)
-            table[i * slots + s] = jnp.where(s < count, at, nothing)
+            at = jnp.where(s < count, at_x * pitch + at_y, nothing)
+            table[i * slots + s] = at
+            if closing:
+                k = final.index((x, y))
+                late_at = (0 if x == 0 else cx + 1) * pitch + final_y + 1
+                is_late = at == late_at
+                sooner[k * slots + s] = jnp.where(is_late, nothing, at)
+                late_slot = jnp.where(is_late, s, late_slot)
+                late_place = jnp.where(is_late, late_at, late_place)
             entry = landed[i, s]
             high = entry.astype(BF16)
-            upper[i, s * block : (s + 1) * block] = high
-            lower[i, s * block : (s + 1) * block] = (
+            upper[i, s] = high
+            lower[i, s] = (
                 entry - high.astype(F32)
             ).astype(BF16)
-
-    def advance(step, x, y):
+        if closing:
+            k = final.index((x, y))
+            late[2 * k], late[2 * k + 1] = late_slot, late_place
+
+    def split_dot(lhs, rhs):
+        product = jnp.dot(lhs, rhs, preferred_element_type=F32)
+        return product[:width, :block] + (
+            product[width:, :block] + product[:width, block:] + product[width:, block:]
+        )
+
+    def gathered(step, x, y, entries, first):
         i = x * cy + y
         field = fields[step % 2]
         lhs = jnp.concatenate(
             [
-                field[jnp.minimum(jnp.maximum(table[i * slots + s], 0), nothing)]
+                field[jnp.minimum(jnp.maximum(entries[first + s], 0), nothing)]
                 for s in range(slots)
             ],
             axis=1,
         )
-        rhs = jnp.concatenate([upper[i], lower[i]], axis=1)
-        product = jnp.dot(lhs, rhs, preferred_element_type=F32)
-        value = product[:width, :block] + (
-            product[width:, :block] + product[:width, block:] + product[width:, block:]
-        )
-        if step:
-            value = 2.0 * value - vectors[step - 1][x, y]
-        vectors[step + 1][x, y] = value
-        if step + 1 < STEPS:
-            put(fields[(step + 1) % 2], (x + 1) * pitch + y + 1, value)
+        high = upper[i].reshape(slots * block, block)
+        low = lower[i].reshape(slots * block, block)
+        value = split_dot(lhs, jnp.concatenate([high, low], axis=1))
+        return 2.0 * value - vectors[step - 1][x, y] if step else value
+
+    def meet(x, y, value):
         start_vector = v0[x, y]
         first_re, first_im = start_vector[:half], start_vector[half:]
         other_re, other_im = value[:half], value[half:]
@@ -232,6 +257,35 @@
             first_re * other_re + first_im * other_im,
             first_re * other_im - first_im * other_re,
         )
+
+    def add_up(step, found):
+        low = step * width
+        sums[low : low + half] += sum(real for real, _ in found)
+        sums[low + half : low + width] += sum(imag for _, imag in found)
+
+    def advance(step, x, y):
+        value = gathered(step, x, y, table, (x * cy + y) * slots)
+        vectors[step + 1][x, y] = value
+        if step + 1 < STEPS:
+            put(fields[(step + 1) % 2], (x + 1) * pitch + y + 1, value)
+        return meet(x, y, value)
+
+    def sooner_part():
+        for k, (x, y) in enumerate(final):
+            last[x, y] = gathered(STEPS - 1, x, y, sooner, k * slots)
+
+    def late_part():
+        found = []
+        field = fields[(STEPS - 1) % 2]
+        for k, (x, y) in enumerate(final):
+            i = x * cy + y
+            slot = jnp.minimum(jnp.maximum(late[2 * k], 0), slots - 1)
+            place = jnp.minimum(jnp.maximum(late[2 * k + 1], 0), nothing)
+            rhs = jnp.concatenate([upper[i, slot], lower[i, slot]], axis=1)
+            value = last[x, y] + 2.0 * split_dot(field[place], rhs)
+            last[x, y] = value
+            found.append(meet(x, y, value))
+        add_up(STEPS - 1, found)
 
     def run(step, place, first, count, unroll):
         def body(k):
@@ -244,9 +298,7 @@
                 if step == 0:
                     prepare(x, y)
                 found.append(advance(step, x, y))
-            low = step * width
-            sums[low : low + half] += sum(real for real, _ in found)
-            sums[low + half : low + width] += sum(imag for _, imag in found)
+            add_up(step, found)
 
         if count == unroll:
             body(0)
@@ -301,6 +353,10 @@
         if more:
             start(y_middles(step + 1))
         for group, ys in enumerate(ready):
+            closing = not more and group + 1 == len(ready)
+            if closing:
+                sooner_part()
+                ring_x[me_x, :, : step * width] = row_sums(0, step * width)
             arrive(x_copies(step, order[group + 2]))
             put_x(step, order[group + 2])
             if group < 2:
@@ -308,7 +364,10 @@
                 arrive(corner_copies(step, side))
                 for end in range(2):
                     put_y(step, side, end * (cx + 1), 2 * end)
-            run(step, rim_x(step, ys), 0, 2 * len(ys), 2 * len(ys))
+            if closing:
+                late_part()
+            else:
+                run(step, rim_x(step, ys), 0, 2 * len(ys), 2 * len(ys))
             if more:
                 if len(ys) > 1:
                     ys = ys[::-1]
@@ -317,18 +376,14 @@
                 if group < 2:
                     start(y_ends(step + 1, 1 if mirror(step, ys[0]) == 0 else 0))
 
-    found = lax.dot_general(
-        jnp.ones((8, block), F32),
-        sums[...],
-        (((1,), (1,)), ((), ())),
-        precision=lax.Precision.HIGHEST,
-        preferred_element_type=F32,
-    )[0:1]
+    low = (STEPS - 1) * width
+    ring_x[me_x, :, low:] = row_sums(low, width)
     for name, size, me, ring, sent, got in (
         (name_x, size_x, me_x, ring_x, sum_send_x, sum_recv_x),
         (name_y, size_y, me_y, ring_y, sum_send_y, sum_recv_y),
     ):
-        ring[me] = found
+        if ring is ring_y:
+            ring[me] = found
         copies = [
             pltpu.make_async_remote_copy(
                 src_ref=ring.at[me],
@@ -346,7 +401,11 @@
         found = ring[0]
         for j in range(1, size):
             found = found + ring[j]
-    total[...] = found
+    scale = 1.0 / math.sqrt(total_x * total_y * block)
+    for part in range(2 * STEPS):
+        total[part // 2, part % 2 : part % 2 + 1] = (
+            found[:, part * half : (part + 1) * half] * scale
+        )
     for step in range(STEPS):
         for y in wire:
             for copy in x_copies(step, y):
@@ -358,18 +417,14 @@
             copy.wait_send()
 
 
-def finish(scale, last, found, out, total, sem):
+def finish(last, total, last_out, total_out, sem):
+    cx = last.shape[0]
     copies = [
-        pltpu.make_async_copy(last.at[x], out.at[x], sem.at[x])
-        for x in range(last.shape[0])
+        pltpu.make_async_copy(last.at[x], last_out.at[x], sem.at[x]) for x in range(cx)
     ]
+    copies.append(pltpu.make_async_copy(total, total_out, sem.at[cx]))
     for copy in copies:
         copy.start()
-    half = total.shape[2]
-    for step in range(STEPS):
-        for part in range(2):
-            low = (2 * step + part) * half
-            total[step, part : part + 1] = found[:, low : low + half] * scale
     for copy in copies:
         copy.wait()
 
@@ -379,7 +434,6 @@
     cx, cy, width, block = probes.shape
     slots = pair_blocks.shape[2]
     cells = cx * cy
-    total_x, total_y = cx * size_x, cy * size_y
     rows = STEPS * width
     halo = (width, block)
     hbm = pl.BlockSpec(memory_space=pltpu.HBM)
@@ -390,7 +444,7 @@
         functools.partial(kernel, axes),
         out_shape=(
             pltpu.VMEM(probes.shape, F32),
-            pltpu.VMEM((1, rows), F32),
+            pltpu.VMEM((STEPS, 2, width // 2), F32),
         ),
         in_specs=[hbm] * 5,
         out_specs=(vmem, vmem),
@@ -406,12 +460,14 @@
             pltpu.VMEM(((cx + 2) * (cy + 2) + 1, 2 * width, block), BF16),
             pltpu.VMEM(((cx + 2) * (cy + 2) + 1, 2 * width, block), BF16),
             pltpu.VMEM((cells, slots, block, block), F32),
-            pltpu.VMEM((cells, slots * block, block), BF16),
-            pltpu.VMEM((cells, slots * block, block), BF16),
+            pltpu.VMEM((cells, slots, block, block), BF16),
+            pltpu.VMEM((cells, slots, block, block), BF16),
             pltpu.VMEM((rows, block), F32),
             pltpu.VMEM((size_x, 1, rows), F32),
             pltpu.VMEM((size_y, 1, rows), F32),
             pltpu.SMEM((cells * slots,), jnp.int32),
+            pltpu.SMEM((2 * cy * slots,), jnp.int32),
+            pltpu.SMEM((4 * cy,), jnp.int32),
             pltpu.VMEM((2, 16, block), F32),
             dma(()),
             dma((3,)),
@@ -427,16 +483,15 @@
             collective_id=0, has_side_effects=True, vmem_limit_bytes=60_000_000
         ),
     )(partners, counts, kpoint, probes, pair_blocks)
-    scale = 1.0 / math.sqrt(total_x * total_y * block)
     return pl.pallas_call(
-        functools.partial(finish, scale),
+        finish,
         out_shape=(
             jax.ShapeDtypeStruct(probes.shape, F32),
             jax.ShapeDtypeStruct((STEPS, 2, width // 2), F32),
         ),
         in_specs=[vmem, vmem],
-        out_specs=(hbm, vmem),
-        scratch_shapes=[dma((cx,))],
+        out_specs=(hbm, hbm),
+        scratch_shapes=[dma((cx + 1,))],
     )(*(pltpu.with_memory_space_constraint(part, pltpu.VMEM) for part in (last, found)))
 
 

time: 45 us -> 43.7 us (0.971)
  Pallas kernels: 44.2 us -> 42.9 us
    pallas_call x1, Pallas kernels: 42.6 us -> 41.9 us  [shards(): pl.pallas_call(functools.partial(kernel, axes), out_shape=(pltpu.VMEM(pro...]
    pallas_call x1, Pallas kernels: 1.63 us -> 1.07 us  [shards(): pl.pallas_call(finish, out_shape=(jax.ShapeDtypeStruct(probes.shape, F32)...]
where the time goes in v3:
time: 43.7 us; the launch traced here: 43.6 us
  Pallas kernels  42.9 us (98%)
  between operations  0.64 us (1%)
    pallas_call x1, Pallas kernels, shards(): pl.pallas_call(functools.partial(kernel, axes), out_shape=(pltpu.VMEM(pro...  41.9 us
    pallas_call x1, Pallas kernels, shards(): pl.pallas_call(finish, out_shape=(jax.ShapeDtypeStruct(probes.shape, F32)...  1.07 us

profile of v3, /device:TPU:0, one launch (start us, length us, event | category | flops | bytes accessed | tf_op | source)
XLA Modules:
  0.0 43.6 jit_solution(628397858020158164)
XLA Ops:
  0.6 41.9 %shard_map.68 = (f32[6,6,64,128]{3,2,1,0:T(8,128)S(1)}, f32[3,2,32]{2,1,0:T(2,128)S(1)}) custom-call(s32[6,6,9]{2,1,0:T(8,128)} %partners_hbm.1, s32[6,6]{1,0:T(8,128)} %counts_hbm.1, f32[2]{0:T(128)} %kpoint_hbm.1, f32[6,6,64,128]{3,2,1,0:T(8,128)} %v0_hbm.1, f32[6,6,9,128,128]{4,3,2,1,0:T(8,128)} %blocks_hbm.1), custom_call_target="tpu_custom_call" | custom-call | tf_op jit(solution)/shard_map/pallas_call | solution.py:443
  42.5 1.1 %shard_map.69 = (f32[6,6,64,128]{3,2,1,0:T(8,128)}, f32[3,2,32]{2,1,0:T(2,128)}) custom-call(f32[6,6,64,128]{3,2,1,0:T(8,128)S(1)} %get-tuple-element.4.last, f32[3,2,32]{2,1,0:T(2,128)S(1)} %get-tuple-element.5.total), custom_call_target="tpu_custom_call" | custom-call | tf_op jit(solution)/shard_map/pallas_call | solution.py:486

commit v4 on v3

--- a/solution.py
+++ b/solution.py
@@ -14,9 +14,9 @@
 
 
 def kernel(
-    axes, partners_hbm, counts_hbm, kpoint_hbm, v0_hbm, blocks_hbm, last, total,
-    partners, counts, kpoint, v0, v1, v2, halo_x, halo_y, field_a, field_b, landed, upper, lower, sums, ring_x, ring_y, table, sooner, late, turns,
-    v0_sem, small_sem, land_sem, send_sem, recv_sem, sum_send_x, sum_recv_x, sum_send_y, sum_recv_y,
+    axes, direct, partners_hbm, counts_hbm, kpoint_hbm, v0_hbm, blocks_hbm, last, total,
+    partners, counts, kpoint, v0, v1, v2, halo_x, halo_y, field_a, field_b, landed, upper, lower, sums, gather, ring, table, sooner, late, turns,
+    v0_sem, small_sem, land_sem, send_sem, recv_sem, sum_send, sum_recv,
 ):
     (name_x, size_x), (name_y, size_y) = axes
     cx, cy, width, block = v0.shape
@@ -356,7 +356,7 @@
             closing = not more and group + 1 == len(ready)
             if closing:
                 sooner_part()
-                ring_x[me_x, :, : step * width] = row_sums(0, step * width)
+                gather[..., : step * width] = row_sums(0, step * width)
             arrive(x_copies(step, order[group + 2]))
             put_x(step, order[group + 2])
             if group < 2:
@@ -377,30 +377,45 @@
                     start(y_ends(step + 1, 1 if mirror(step, ys[0]) == 0 else 0))
 
     low = (STEPS - 1) * width
-    ring_x[me_x, :, low:] = row_sums(low, width)
-    for name, size, me, ring, sent, got in (
-        (name_x, size_x, me_x, ring_x, sum_send_x, sum_recv_x),
-        (name_y, size_y, me_y, ring_y, sum_send_y, sum_recv_y),
-    ):
-        if ring is ring_y:
-            ring[me] = found
-        copies = [
-            pltpu.make_async_remote_copy(
-                src_ref=ring.at[me],
-                dst_ref=ring.at[me],
-                send_sem=sent.at[j],
-                recv_sem=got.at[j],
-                device_id={name: lax.rem(me + j, size)},
-                device_id_type=MESH,
+    gather[..., low:] = row_sums(low, width)
+    if direct:
+        stages = (("both", size_x * size_y),)
+    else:
+        stages = ((name_x, size_x), (name_y, size_y))
+    found = gather[...]
+    first = 0
+    for name, size in stages:
+        if name == "both":
+            me = me_x * size_y + me_y
+        else:
+            me = me_x if name == name_x else me_y
+        ring[first + me] = found
+        copies = []
+        for j in range(size - 1, 0, -1):
+            if name == "both":
+                peer = {
+                    name_x: lax.rem(me_x + j // size_y, size_x),
+                    name_y: lax.rem(me_y + j % size_y, size_y),
+                }
+            else:
+                peer = {name: lax.rem(me + j, size)}
+            copies.append(
+                pltpu.make_async_remote_copy(
+                    src_ref=ring.at[first + me],
+                    dst_ref=ring.at[first + me],
+                    send_sem=sum_send.at[first + j],
+                    recv_sem=sum_recv.at[first + j],
+                    device_id=peer,
+                    device_id_type=MESH,
+                )
             )
-            for j in range(1, size)
-        ]
         start(copies)
         for copy in copies:
             copy.wait()
-        found = ring[0]
+        found = ring[first]
         for j in range(1, size):
-            found = found + ring[j]
+            found = found + ring[first + j]
+        first += size
     scale = 1.0 / math.sqrt(total_x * total_y * block)
     for part in range(2 * STEPS):
         total[part // 2, part % 2 : part % 2 + 1] = (
@@ -440,8 +455,10 @@
     vmem = pl.BlockSpec(memory_space=pltpu.VMEM)
     dma = pltpu.SemaphoreType.DMA
     kinds = 2 * cy + 10
+    direct = size_x // 2 < STEPS
+    peers = size_x * size_y if direct else size_x + size_y
     last, found = pl.pallas_call(
-        functools.partial(kernel, axes),
+        functools.partial(kernel, axes, direct),
         out_shape=(
             pltpu.VMEM(probes.shape, F32),
             pltpu.VMEM((STEPS, 2, width // 2), F32),
@@ -463,8 +480,8 @@
             pltpu.VMEM((cells, slots, block, block), BF16),
             pltpu.VMEM((cells, slots, block, block), BF16),
             pltpu.VMEM((rows, block), F32),
-            pltpu.VMEM((size_x, 1, rows), F32),
-            pltpu.VMEM((size_y, 1, rows), F32),
+            pltpu.VMEM((1, rows), F32),
+            pltpu.VMEM((peers, 1, rows), F32),
             pltpu.SMEM((cells * slots,), jnp.int32),
             pltpu.SMEM((2 * cy * slots,), jnp.int32),
             pltpu.SMEM((4 * cy,), jnp.int32),
@@ -474,10 +491,8 @@
             dma((cells,)),
             dma((STEPS, kinds)),
             dma((STEPS, kinds)),
-            dma((size_x,)),
-            dma((size_x,)),
-            dma((size_y,)),
-            dma((size_y,)),
+            dma((peers,)),
+            dma((peers,)),
         ],
         compiler_params=pltpu.CompilerParams(
             collective_id=0, has_side_effects=True, vmem_limit_bytes=60_000_000

time: 43.7 us -> 42.5 us (0.973)
  Pallas kernels: 42.9 us -> 41.7 us
    pallas_call x1, Pallas kernels: 41.9 us -> 40.6 us  [shards(): pl.pallas_call(functools.partial(kernel, axes, direct), out_shape=(pltpu....]
where the time goes in v4:
time: 42.5 us; the launch traced here: 42.3 us
  Pallas kernels  41.7 us (98%)
  between operations  0.64 us (2%)
    pallas_call x1, Pallas kernels, shards(): pl.pallas_call(functools.partial(kernel, axes, direct), out_shape=(pltpu....  40.6 us
    pallas_call x1, Pallas kernels, shards(): pl.pallas_call(finish, out_shape=(jax.ShapeDtypeStruct(probes.shape, F32)...  1.07 us

profile of v4, /device:TPU:0, one launch (start us, length us, event | category | flops | bytes accessed | tf_op | source)
XLA Modules:
  0.0 42.3 jit_solution(17711009158709238095)
XLA Ops:
  0.6 40.6 %shard_map.68 = (f32[6,6,64,128]{3,2,1,0:T(8,128)S(1)}, f32[3,2,32]{2,1,0:T(2,128)S(1)}) custom-call(s32[6,6,9]{2,1,0:T(8,128)} %partners_hbm.1, s32[6,6]{1,0:T(8,128)} %counts_hbm.1, f32[2]{0:T(128)} %kpoint_hbm.1, f32[6,6,64,128]{3,2,1,0:T(8,128)} %v0_hbm.1, f32[6,6,9,128,128]{4,3,2,1,0:T(8,128)} %blocks_hbm.1), custom_call_target="tpu_custom_call" | custom-call | tf_op jit(solution)/shard_map/pallas_call | solution.py:460
  41.3 1.1 %shard_map.69 = (f32[6,6,64,128]{3,2,1,0:T(8,128)}, f32[3,2,32]{2,1,0:T(2,128)}) custom-call(f32[6,6,64,128]{3,2,1,0:T(8,128)S(1)} %get-tuple-element.4.last, f32[3,2,32]{2,1,0:T(2,128)S(1)} %get-tuple-element.5.total), custom_call_target="tpu_custom_call" | custom-call | tf_op jit(solution)/shard_map/pallas_call | solution.py:501

commit v5 on v4

--- a/solution.py
+++ b/solution.py
@@ -115,6 +115,16 @@
             for side in range(2)
         ]
 
+    def start_x(step, y):
+        for side in (1 - lax.rem(me_x, 2), lax.rem(me_x, 2)):
+            remote(
+                step,
+                2 * y + side,
+                source(step).at[(1 - side) * (cx - 1), y],
+                halo_x.at[step, side, y],
+                {name_x: lax.rem(me_x + 1 + side * (size_x - 2), size_x)},
+            ).start()
+
     def y_copy(step, side, x, length):
         return remote(
             step,
@@ -151,30 +161,39 @@
             copy.wait_recv()
 
     def row_sums(first, length):
-        return lax.dot_general(
-            jnp.ones((8, block), F32),
-            sums[first : first + length],
-            (((1,), (1,)), ((), ())),
-            precision=lax.Precision.HIGHEST,
+        value = sums[first : first + length]
+        parts = []
+        for _ in range(3):
+            part = value.astype(BF16)
+            parts.append(part)
+            value = value - part.astype(F32)
+        whole = jnp.dot(
+            jnp.concatenate(parts, axis=1),
+            jnp.ones((3 * block, block), BF16),
             preferred_element_type=F32,
-        )[0:1]
+        )
+        line = lax.broadcasted_iota(jnp.int32, (length, block), 0)
+        lane = lax.broadcasted_iota(jnp.int32, (length, block), 1)
+        row = jnp.sum(jnp.where(line == lane, whole, 0.0), axis=0, keepdims=True)
+        return row[:, :length]
+
+    def parts(value):
+        high = value.astype(BF16)
+        return high, (value - high.astype(F32)).astype(BF16)
 
     def put(field, position, value):
-        high = value.astype(BF16)
-        field[position, :width] = high
-        field[position, width:] = (value - high.astype(F32)).astype(BF16)
-
-    def put_turned(field, position, value, at_x, at_y):
+        field[position, :width], field[position, width:] = parts(value)
+
+    def turned(value, at_x, at_y):
         entry = at_x * 3 + at_y
         cosine, sine = turns[0, entry : entry + 1], turns[1, entry : entry + 1]
         real, imag = value[:half], value[half:]
-        put(
-            field,
-            position,
-            jnp.concatenate(
-                [cosine * real - sine * imag, sine * real + cosine * imag], axis=0
-            ),
-        )
+        return jnp.concatenate(
+            [cosine * real - sine * imag, sine * real + cosine * imag], axis=0
+        )
+
+    def put_turned(field, position, value, at_x, at_y):
+        put(field, position, turned(value, at_x, at_y))
 
     def put_x(step, y):
         for side in range(2):
@@ -275,14 +294,18 @@
             last[x, y] = gathered(STEPS - 1, x, y, sooner, k * slots)
 
     def late_part():
+        halves = [
+            parts(turned(halo_x[STEPS - 1, side, final_y], 2 * side, 1))
+            for side in range(2)
+        ]
         found = []
-        field = fields[(STEPS - 1) % 2]
         for k, (x, y) in enumerate(final):
             i = x * cy + y
             slot = jnp.minimum(jnp.maximum(late[2 * k], 0), slots - 1)
-            place = jnp.minimum(jnp.maximum(late[2 * k + 1], 0), nothing)
             rhs = jnp.concatenate([upper[i, slot], lower[i, slot]], axis=1)
-            value = last[x, y] + 2.0 * split_dot(field[place], rhs)
+            lhs = jnp.concatenate(halves[1 if x else 0], axis=0)
+            twice = jnp.where(late[2 * k + 1] < nothing, 2.0, 0.0).astype(F32)
+            value = last[x, y] + twice * split_dot(lhs, rhs)
             last[x, y] = value
             found.append(meet(x, y, value))
         add_up(STEPS - 1, found)
@@ -306,7 +329,7 @@
             pl.loop(0, count // unroll)(body)
 
     for y in wire:
-        start(x_copies(0, y))
+        start_x(0, y)
     start(y_middles(0) + y_ends(0, 0) + y_ends(0, 1))
     sums[...] = jnp.zeros_like(sums)
     for field in fields:
@@ -356,9 +379,11 @@
             closing = not more and group + 1 == len(ready)
             if closing:
                 sooner_part()
-                gather[..., : step * width] = row_sums(0, step * width)
+                for k in range(step):
+                    gather[..., k * width : (k + 1) * width] = row_sums(k * width, width)
             arrive(x_copies(step, order[group + 2]))
-            put_x(step, order[group + 2])
+            if not closing:
+                put_x(step, order[group + 2])
             if group < 2:
                 side = 1 - near if group == 0 else near
                 arrive(corner_copies(step, side))
@@ -372,7 +397,7 @@
                 if len(ys) > 1:
                     ys = ys[::-1]
                 for y in ys:
-                    start(x_copies(step + 1, mirror(step, y)))
+                    start_x(step + 1, mirror(step, y))
                 if group < 2:
                     start(y_ends(step + 1, 1 if mirror(step, ys[0]) == 0 else 0))
 
@@ -433,11 +458,10 @@
 
 
 def finish(last, total, last_out, total_out, sem):
-    cx = last.shape[0]
     copies = [
-        pltpu.make_async_copy(last.at[x], last_out.at[x], sem.at[x]) for x in range(cx)
+        pltpu.make_async_copy(total, total_out, sem.at[0]),
+        pltpu.make_async_copy(last, last_out, sem.at[1]),
     ]
-    copies.append(pltpu.make_async_copy(total, total_out, sem.at[cx]))
     for copy in copies:
         copy.start()
     for copy in copies:
@@ -506,7 +530,7 @@
         ),
         in_specs=[vmem, vmem],
         out_specs=(hbm, hbm),
-        scratch_shapes=[dma((cx + 1,))],
+        scratch_shapes=[dma((2,))],
     )(*(pltpu.with_memory_space_constraint(part, pltpu.VMEM) for part in (last, found)))
 
 

time: 42.5 us -> 41.9 us (0.986)
  Pallas kernels: 41.7 us -> 41.1 us
    pallas_call x1, Pallas kernels: 40.6 us -> 40 us  [shards(): pl.pallas_call(functools.partial(kernel, axes, direct), out_shape=(pltpu....]
where the time goes in v5:
time: 41.9 us; the launch traced here: 41.7 us
  Pallas kernels  41.1 us (98%)
  between operations  0.64 us (2%)
    pallas_call x1, Pallas kernels, shards(): pl.pallas_call(functools.partial(kernel, axes, direct), out_shape=(pltpu....  40 us
    pallas_call x1, Pallas kernels, shards(): pl.pallas_call(finish, out_shape=(jax.ShapeDtypeStruct(probes.shape, F32)...  1.04 us

profile of v5, /device:TPU:0, one launch (start us, length us, event | category | flops | bytes accessed | tf_op | source)
XLA Modules:
  0.0 41.7 jit_solution(129372807292744273)
XLA Ops:
  0.6 40.0 %shard_map.68 = (f32[6,6,64,128]{3,2,1,0:T(8,128)S(1)}, f32[3,2,32]{2,1,0:T(2,128)S(1)}) custom-call(s32[6,6,9]{2,1,0:T(8,128)} %partners_hbm.1, s32[6,6]{1,0:T(8,128)} %counts_hbm.1, f32[2]{0:T(128)} %kpoint_hbm.1, f32[6,6,64,128]{3,2,1,0:T(8,128)} %v0_hbm.1, f32[6,6,9,128,128]{4,3,2,1,0:T(8,128)} %blocks_hbm.1), custom_call_target="tpu_custom_call" | custom-call | tf_op jit(solution)/shard_map/pallas_call | solution.py:484
  40.7 1.0 %shard_map.69 = (f32[6,6,64,128]{3,2,1,0:T(8,128)}, f32[3,2,32]{2,1,0:T(2,128)}) custom-call(f32[6,6,64,128]{3,2,1,0:T(8,128)S(1)} %get-tuple-element.4.last, f32[3,2,32]{2,1,0:T(2,128)S(1)} %get-tuple-element.5.total), custom_call_target="tpu_custom_call" | custom-call | tf_op jit(solution)/shard_map/pallas_call | solution.py:525

commit v6 on v5

--- a/solution.py
+++ b/solution.py
@@ -330,7 +330,7 @@
 
     for y in wire:
         start_x(0, y)
-    start(y_middles(0) + y_ends(0, 0) + y_ends(0, 1))
+    start(y_ends(0, 0) + y_ends(0, 1) + y_middles(0))
     sums[...] = jnp.zeros_like(sums)
     for field in fields:
         field[nothing] = jnp.zeros_like(field[nothing])
@@ -418,18 +418,22 @@
         copies = []
         for j in range(size - 1, 0, -1):
             if name == "both":
+                step_x = (j // size_y) * (1 + lax.rem(me_x, 2) * (size_x - 2))
+                step_x = lax.rem(step_x, size_x)
                 peer = {
-                    name_x: lax.rem(me_x + j // size_y, size_x),
+                    name_x: lax.rem(me_x + step_x, size_x),
                     name_y: lax.rem(me_y + j % size_y, size_y),
                 }
+                offset = step_x * size_y + j % size_y
             else:
                 peer = {name: lax.rem(me + j, size)}
+                offset = j
             copies.append(
                 pltpu.make_async_remote_copy(
                     src_ref=ring.at[first + me],
                     dst_ref=ring.at[first + me],
-                    send_sem=sum_send.at[first + j],
-                    recv_sem=sum_recv.at[first + j],
+                    send_sem=sum_send.at[first + offset],
+                    recv_sem=sum_recv.at[first + offset],
                     device_id=peer,
                     device_id_type=MESH,
                 )

time: 41.9 us -> 41.7 us (level)
  no operation moved by 1% of the time
where the time goes in v6:
time: 41.7 us; the launch traced here: 41.6 us
  Pallas kernels  41 us (98%)
  between operations  0.64 us (2%)
    pallas_call x1, Pallas kernels, shards(): pl.pallas_call(functools.partial(kernel, axes, direct), out_shape=(pltpu....  39.9 us
    pallas_call x1, Pallas kernels, shards(): pl.pallas_call(finish, out_shape=(jax.ShapeDtypeStruct(probes.shape, F32)...  1.04 us

profile of v6, /device:TPU:0, one launch (start us, length us, event | category | flops | bytes accessed | tf_op | source)
XLA Modules:
  0.0 41.6 jit_solution(17686603041784770870)
XLA Ops:
  0.6 39.9 %shard_map.68 = (f32[6,6,64,128]{3,2,1,0:T(8,128)S(1)}, f32[3,2,32]{2,1,0:T(2,128)S(1)}) custom-call(s32[6,6,9]{2,1,0:T(8,128)} %partners_hbm.1, s32[6,6]{1,0:T(8,128)} %counts_hbm.1, f32[2]{0:T(128)} %kpoint_hbm.1, f32[6,6,64,128]{3,2,1,0:T(8,128)} %v0_hbm.1, f32[6,6,9,128,128]{4,3,2,1,0:T(8,128)} %blocks_hbm.1), custom_call_target="tpu_custom_call" | custom-call | tf_op jit(solution)/shard_map/pallas_call | solution.py:488
  40.6 1.0 %shard_map.69 = (f32[6,6,64,128]{3,2,1,0:T(8,128)}, f32[3,2,32]{2,1,0:T(2,128)}) custom-call(f32[6,6,64,128]{3,2,1,0:T(8,128)S(1)} %get-tuple-element.4.last, f32[3,2,32]{2,1,0:T(2,128)S(1)} %get-tuple-element.5.total), custom_call_target="tpu_custom_call" | custom-call | tf_op jit(solution)/shard_map/pallas_call | solution.py:529
